TPU v7x, 512 devices: a whole 4x4x16 slice. The times are simulated.
512 devices in a mesh: seq: 32 (over x, y, core), head: 16 (over z).
Axes of the slice: x: 4, y: 4, z: 16, core: 2. Of those that a mesh axis runs over, the one named last changes fastest.
Arguments:
- queries: bfloat16 [32768, 4096], P('seq', 'head'), may hold values from -6 to 6
- keys: bfloat16 [32768, 4096], P('seq', 'head'), may hold values from -6 to 6
- values: bfloat16 [32768, 4096], P('seq', 'head'), may hold values from -6 to 6
- out_weight: bfloat16 [4096, 4096], P(None, 'head'), may hold values from -0.09375 to 0.09375
Outputs:
- output: bfloat16 [32768, 4096], P('seq', 'head')
All inputs are finite; a program needn't handle non-finite values.
Results may differ from a plain program's by a relative error of at most 0.0058.
Values may be sent and summed in bfloat16 or wider, within the bound.
A program may use at most 64 MiB of HBM per device.

v0:
```python
import jax
import jax.numpy as jnp
from jax import lax
from jax.sharding import PartitionSpec as P

HD = 128
BLOCK = 1024


def prefix_2(value, axis, join, neutral):
    count, mine = (lax.axis_size(axis), lax.axis_index(axis))
    pieces = lax.all_gather(value, axis)
    running = jnp.full_like(value, 0) + jnp.asarray(neutral, value.dtype)

    def step(position, running):
        longer = join(running, pieces[position])
        return jnp.where(position < mine, longer, running)

    return lax.fori_loop(0, count - 1, step, running)


def add_states(earlier, later):
    return earlier + later


def per_device(queries, keys, values, out_weight):
    tok_rows = queries.shape[0]
    local_heads = queries.shape[1] // HD
    blocks_count = tok_rows // BLOCK
    block_shape = (blocks_count, BLOCK, local_heads, HD)
    query_blocks = queries.reshape(block_shape)
    key_blocks = keys.reshape(block_shape)
    value_blocks = values.reshape(block_shape)
    block_states = jnp.einsum(
        "cthd,cthe->chde", key_blocks, value_blocks, preferred_element_type=jnp.float32
    )
    own_state = jnp.sum(block_states, 0)
    prefix = prefix_2(own_state, "seq", add_states, jnp.zeros_like(own_state))
    earlier = prefix[None] + jnp.cumsum(block_states, 0) - block_states
    causal = jnp.arange(BLOCK)[:, None] >= jnp.arange(BLOCK)[None, :]

    def one_block(inputs):
        query_rows, key_rows, value_rows, carried = inputs
        scores = jnp.einsum(
            "thd,shd->hts", query_rows, key_rows, preferred_element_type=jnp.float32
        )
        scores = jnp.where(causal[None], scores, 0.0).astype(jnp.bfloat16)
        attended = jnp.einsum(
            "hts,shd->thd", scores, value_rows, preferred_element_type=jnp.float32
        )
        attended = attended + jnp.einsum(
            "thd,hde->the",
            query_rows,
            carried.astype(jnp.bfloat16),
            preferred_element_type=jnp.float32,
        )
        normed = attended * lax.rsqrt(jnp.mean(attended * attended, -1, keepdims=True) + 1e-06)
        return normed.astype(jnp.bfloat16).reshape(BLOCK, local_heads * HD)

    mixed_heads = lax.map(one_block, (query_blocks, key_blocks, value_blocks, earlier)).reshape(
        tok_rows, local_heads * HD
    )
    output = jnp.dot(
        lax.all_gather(mixed_heads, "head", axis=1, tiled=True),
        out_weight,
        preferred_element_type=jnp.float32,
    )
    return output.astype(jnp.bfloat16)


def solution(mesh):
    return jax.shard_map(
        per_device,
        mesh=mesh,
        in_specs=(P("seq", "head"), P("seq", "head"), P("seq", "head"), P(None, "head")),
        out_specs=P("seq", "head"),
        check_vma=False,
    )
```

profile of v0, /device:TPU:1, one launch (start us, length us, event | category | flops | bytes accessed | tf_op | source)
XLA Modules:
  0.0 229.1 jit_solution(4268179932716911457)
XLA Ops:
  6.5 0.0 copy-start
  6.5 0.0 all-gather.6.cloned.1.call-start
  6.5 1.4 copy.16
  7.9 0.0 copy-start.2
  8.0 2.2 fusion.8
  10.2 0.0 all-gather.6.cloned.1.call-update
  10.2 0.0 all-gather.4.cloned.1.call-start
  10.2 0.0 copy-done.2
  10.3 0.3 iota_compare_fusion
  10.6 0.0 copy-start.1
  10.6 5.0 %fusion.6 = f32[1024,2,128]{0,2,1:T(8,128)} fusion(pred[1024,1024]{1,0:T(8,128)(4,1)S(1)} %iota_compare_fusion, bf16[1024,2,128]{0,2,1:T(8,128)(2,1)} %bitcast.47, bf16[1024,256]{1,0:T(8,128)(2,1)} %param.8, bf16[1024,256]{1,0:T(8,128)(2,1)} %param.6), kind=kOutput, calls=%fused_computation.9 | convolution fusion | flops 1077936128 | bytes 3670016 | tf_op jit(solution)/shard_map/while/body/eval_jaxpr/hts,shd->thd/dot_general | solution.py:48
  15.6 62.0 %all-gather.6.cloned.1.call-done = f32[64,128,128]{2,1,0:T(8,128)} async-done(((f32[2,128,128]{2,1,0:T(8,128)}), f32[64,128,128]{2,1,0:T(8,128)}) %all-gather.6.cloned.1.call-update) | async-done | bytes 4194320 | tf_op jit(solution)/shard_map/all_gather | solution.py:12
  77.6 30.1 %while.18 = (s32[]{:T(128)}, f32[2,128,128]{2,1,0:T(8,128)S(1)}, s32[]{:T(128)}, f32[32,2,128,128]{3,2,1,0:T(8,128)}, s32[]{:T(128)}, /*index=5*/s32[]{:T(128)}) while((s32[]{:T(128)}, f32[2,128,128]{2,1,0:T(8,128)S(1)}, s32[]{:T(128)}, f32[32,2,128,128]{3,2,1,0:T(8,128)}, s32[]{:T(128)}, /*index=5*/s32[]{:T(128)}) %tuple.42), condition=%wide.region_1.2_spmd.clone, body=%wide.region_0.0_spmd.clone.sunk | while | flops 98308 | bytes 393317 | solution.py:19
  77.6 0.9 add_select_fusion.2
  78.6 0.9 add_select_fusion.2
  79.6 0.9 add_select_fusion.2
  80.5 0.9 add_select_fusion.2
  81.5 0.9 add_select_fusion.2
  82.5 0.9 add_select_fusion.2
  83.5 0.9 add_select_fusion.2
  84.4 0.9 add_select_fusion.2
  85.4 0.9 add_select_fusion.2
  86.4 0.9 add_select_fusion.2
  87.4 0.9 add_select_fusion.2
  88.3 0.9 add_select_fusion.2
  89.3 0.9 add_select_fusion.2
  90.3 0.9 add_select_fusion.2
  91.3 0.9 add_select_fusion.2
  92.2 0.9 add_select_fusion.2
  93.2 0.9 add_select_fusion.2
  94.2 0.9 add_select_fusion.2
  95.1 0.9 add_select_fusion.2
  96.1 0.9 add_select_fusion.2
  97.1 0.9 add_select_fusion.2
  98.1 0.9 add_select_fusion.2
  99.0 0.9 add_select_fusion.2
  100.0 0.9 add_select_fusion.2
  101.0 0.9 add_select_fusion.2
  102.0 0.9 add_select_fusion.2
  102.9 0.9 add_select_fusion.2
  103.9 0.9 add_select_fusion.2
  104.9 0.9 add_select_fusion.2
  105.8 0.9 add_select_fusion.2
  106.8 0.9 add_select_fusion.2
  107.8 0.0 copy-done.1
  107.8 1.7 multiply_reduce_fusion
  109.6 0.9 multiply_convert_fusion
  110.5 0.0 all-gather.4.cloned.1.call-update
  110.5 105.2 %all-gather.4.cloned.1.call-done = bf16[1024,4096]{0,1:T(8,128)(2,1)} async-done(((bf16[1024,256]{0,1:T(8,128)(2,1)}), bf16[1024,4096]{0,1:T(8,128)(2,1)}) %all-gather.4.cloned.1.call-update) | async-done | bytes 8388624 | tf_op jit(solution)/shard_map/all_gather | solution.py:64
  215.7 0.0 copy-done
  215.7 6.6 %convolution_convert_fusion = bf16[1024,256]{1,0:T(8,128)(2,1)} fusion(bf16[1024,4096]{0,1:T(8,128)(2,1)} %all-gather.4.cloned.1.call-done, bf16[4096,256]{1,0:T(8,128)(2,1)S(1)} %copy-done), kind=kOutput, calls=%fused_computation.10 | convolution fusion | flops 2147745792 | bytes 11010048 | tf_op jit(solution)/shard_map/dot_general | solution.py:63
  (2 shorter events, 0.0 us)
Async XLA Ops:
  6.5 209.1 %copy-start = (bf16[4096,256]{1,0:T(8,128)(2,1)S(1)}, bf16[4096,256]{1,0:T(8,128)(2,1)}, u32[]{:S(2)}) copy-start(bf16[4096,256]{1,0:T(8,128)(2,1)} %param.9) | copy-start | bytes 6291460
  6.5 71.1 %all-gather.6.cloned.1.call-start = ((), (), s32[]{:S(2)}) async-start(), calls=%async_computation.1 | async-start | bytes 4325376 | tf_op jit(solution)/shard_map/all_gather | solution.py:12
  7.9 2.3 copy-start.2
  10.2 205.5 %all-gather.4.cloned.1.call-start = ((), (), s32[]{:S(2)}) async-start(), calls=%async_computation | async-start | bytes 8912896 | tf_op jit(solution)/shard_map/all_gather | solution.py:64
  10.6 97.2 %copy-start.1 = (f32[2,128,128]{2,1,0:T(8,128)S(1)}, f32[2,128,128]{2,1,0:T(8,128)}, u32[]{:S(2)}) copy-start(f32[2,128,128]{2,1,0:T(8,128)} %fusion.8) | copy-start | bytes 393220
Sparse Core Ops, SparseCore 0:
  10.5 67.0 all-gather.5
  110.6 105.0 all-gather.3
where the time goes:
time: 230 us; the launch traced here: 229 us
  waiting for transfers between devices  167 us (73%)
  other arithmetic  30.7 us (13%)
  matrix products  15.6 us (7%)
  between operations  13.5 us (6%)
    all_gather x1, waiting for transfers between devices, per_device(): lax.all_gather(mixed_heads, 'head', axis=1, tiled=True)  105 us
    all_gather x1, waiting for transfers between devices, prefix_2(): pieces = lax.all_gather(value, axis)  62 us
    select_n x31, other arithmetic, step(): return jnp.where(position < mine, longer, running)  29.4 us
    dot_general x1, matrix products, per_device(): jnp.dot(lax.all_gather(mixed_heads, 'head', axis=1, tiled=True), out_weig...  6.55 us
    dot_general x1, matrix products, one_block(): jnp.einsum('hts,shd->thd', scores, value_rows, preferred_element_type=jnp...  5.05 us
  transfers between devices with their start and end apart: 2, of which 2 were waited for; matrix products, arithmetic and copies ran while one was open for 2% of the time, Pallas kernels for 0%

commit v1 on v0

v1 whole, which is shorter than its diff:
```python
import jax
import jax.numpy as jnp
from jax import lax
from jax.experimental import pallas as pl
from jax.experimental.pallas import tpu as pltpu
from jax.sharding import PartitionSpec as P

HD = 128
ROWS = 1024
HALF = 512
WIDE = 256
SUB = 256
RING = 16
SIDE = 4
F32 = jnp.float32
BF16 = jnp.bfloat16


def dot(a, b):
    return jnp.dot(a, b, preferred_element_type=F32)


def remote(src, dst, send, recv, where):
    return pltpu.make_async_remote_copy(
        src_ref=src,
        dst_ref=dst,
        send_sem=send,
        recv_sem=recv,
        device_id=where,
        device_id_type=pl.DeviceIdType.MESH,
    )


def kernel(
    q_hbm, k_hbm, v_hbm, w_hbm, out,
    q, k, v, w, intra, acc, mixed,
    s_own, s_send, s_recv, t_own, t_recv, r_own, r_recv, c_own, c_send, c_recv, c_blk,
    in_sems, pair_send, pair_recv, y_send, y_recv, x_send, x_recv, c_sems,
    ra_send, ra_recv, rb_send, rb_recv, la_send, la_recv, lb_send, lb_recv,
):
    seq, z = lax.axis_index("seq"), lax.axis_index("head")
    core, y, x = seq % 2, (seq // 2) % SIDE, seq // (2 * SIDE)
    partner = {"seq": seq + 1 - 2 * core}
    y_peers = [{"seq": (x * SIDE + (y + d) % SIDE) * 2 + core} for d in range(1, SIDE)]
    x_peers = [{"seq": (((x + d) % SIDE) * SIDE + y) * 2 + core} for d in range(1, SIDE)]
    right = {"head": (z + 1) % RING}
    left = {"head": (z + RING - 1) % RING}

    barrier = pltpu.get_barrier_semaphore()
    everyone = [partner, right, left] + y_peers + x_peers
    for who in everyone:
        pl.semaphore_signal(barrier, inc=1, device_id=who, device_id_type=pl.DeviceIdType.MESH)
    loads = [
        pltpu.make_async_copy(src, dst, in_sems.at[i])
        for i, (src, dst) in enumerate(((k_hbm, k), (v_hbm, v), (q_hbm, q), (w_hbm, w)))
    ]
    for load in loads:
        load.start()
    loads[0].wait()
    loads[1].wait()
    states = lax.dot_general(k[...], v[...], (((0,), (0,)), ((), ())), preferred_element_type=F32)
    first, second = states[:HD, :HD], states[HD:, HD:]
    s_own[...] = jnp.where(core == 0, first, second)
    s_send[...] = jnp.where(core == 0, second, first)
    pl.semaphore_wait(barrier, len(everyone))
    pair = remote(s_send, s_recv, pair_send, pair_recv, partner)
    pair.start()

    def intra_part(head, part):
        cols = pl.ds(head * HD, HD)
        rows = pl.ds(part * SUB, SUB)
        width = (part + 1) * SUB
        scores = lax.dot_general(
            q[rows, cols], k[pl.ds(0, width), cols], (((1,), (1,)), ((), ())),
            preferred_element_type=F32,
        )
        query_at = lax.broadcasted_iota(jnp.int32, (SUB, width), 0) + part * SUB
        key_at = lax.broadcasted_iota(jnp.int32, (SUB, width), 1)
        scores = jnp.where(query_at >= key_at, scores, 0.0).astype(BF16)
        intra[rows, cols] = dot(scores, v[pl.ds(0, width), cols])

    loads[2].wait()
    intra_part(0, 0)
    intra_part(1, 0)

    pair.wait()
    t_own[...] = s_own[...] + s_recv[...]
    y_copies = [
        remote(t_own, t_recv.at[d], y_send.at[d], y_recv.at[d], y_peers[d]) for d in range(3)
    ]
    for copy in y_copies:
        copy.start()
    intra_part(0, 1)
    intra_part(1, 1)
    intra_part(0, 2)
    for copy in y_copies:
        copy.wait()
    prefix = jnp.zeros((HD, HD), F32)
    total = t_own[...]
    for d in range(3):
        piece = t_recv[d]
        total = total + piece
        prefix = prefix + jnp.where(d + 1 <= y, piece, 0.0)
    r_own[...] = total
    x_copies = [
        remote(r_own, r_recv.at[d], x_send.at[d], x_recv.at[d], x_peers[d]) for d in range(3)
    ]
    for copy in x_copies:
        copy.start()
    s_send[...] = prefix
    intra_part(1, 2)
    intra_part(0, 3)
    intra_part(1, 3)
    for copy in x_copies:
        copy.wait()
    prefix = s_send[...]
    for d in range(3):
        prefix = prefix + jnp.where(d + 1 <= x, r_recv[d], 0.0)
    from_first = jnp.where(core == 0, s_own[...], s_recv[...])
    longer = prefix + from_first
    c_send[...] = jnp.where(core == 0, longer, prefix).astype(BF16)
    cross = remote(c_send, c_recv, c_sems.at[0], c_sems.at[1], partner)
    cross.start()
    c_own[...] = jnp.where(core == 0, prefix, longer).astype(BF16)
    c_blk[...] = jnp.zeros((WIDE, WIDE), BF16)
    loads[3].wait()
    cross.wait()
    mine, other = c_own[...].astype(F32), c_recv[...].astype(F32)
    c_blk[pl.ds(0, HD), pl.ds(0, HD)] = jnp.where(core == 0, mine, other).astype(BF16)
    c_blk[pl.ds(HD, HD), pl.ds(HD, HD)] = jnp.where(core == 0, other, mine).astype(BF16)

    def piece_at(owner, half):
        return mixed.at[owner, pl.ds(half * HALF, HALF)]

    def hop(owner, half, send, recv, step, where):
        ref = piece_at(owner, half)
        return remote(ref, ref, send.at[step], recv.at[step], where)

    def right_a(step):
        return hop((z + RING - step) % RING, 0, ra_send, ra_recv, step, right)

    def right_b(step):
        return hop((z + RING - step) % RING, 1, rb_send, rb_recv, step, right)

    def left_a(step):
        return hop((z + step) % RING, 0, la_send, la_recv, step, left)

    def left_b(step):
        return hop((z + step) % RING, 1, lb_send, lb_recv, step, left)

    def norm_half(half):
        for part in range(2):
            rows = pl.ds(half * HALF + part * SUB, SUB)
            attended = intra[rows, :] + dot(q[rows, :], c_blk[...])
            for head in range(2):
                own = attended[:, head * HD:(head + 1) * HD]
                scale = lax.rsqrt(jnp.mean(own * own, -1, keepdims=True) + 1e-06)
                mixed[z, rows, pl.ds(head * HD, HD)] = (own * scale).astype(BF16)

    norm_half(0)
    right_a(0).start()
    left_a(0).start()
    norm_half(1)
    left_b(0).start()
    right_b(0).start()

    def weights(owner):
        return w[pl.ds(pl.multiple_of(owner * WIDE, WIDE), WIDE), :]

    acc[...] = dot(mixed[z], weights(z))

    def add(owner, half):
        rows = pl.ds(half * HALF, HALF)
        acc[rows, :] += dot(mixed[owner, rows, :], weights(owner))

    def step_body(step, carry):
        before = (z + 2 * RING - step - 1) % RING
        after = (z + step + 1) % RING
        right_a(step).wait_recv()
        right_a(step + 1).start()
        left_b(step).wait_recv()
        left_b(step + 1).start()
        add(before, 0)
        add(after, 1)
        left_a(step).wait_recv()
        right_b(step).wait_recv()

        @pl.when(step < RING // 2 - 2)
        def _():
            left_a(step + 1).start()
            right_b(step + 1).start()

        add(after, 0)
        add(before, 1)
        return carry

    last = RING // 2 - 1
    lax.fori_loop(0, last, step_body, 0)
    far = (z + RING // 2) % RING
    for half, copy in ((0, right_a(last)), (1, left_b(last))):
        copy.wait_recv()
        rows = pl.ds(half * HALF, HALF)
        out[rows, :] = (acc[rows, :] + dot(mixed[far, rows, :], weights(far))).astype(BF16)

    def drain(step, carry):
        right_a(step).wait_send()
        left_b(step).wait_send()

        @pl.when(step < last)
        def _():
            left_a(step).wait_send()
            right_b(step).wait_send()

        return carry

    lax.fori_loop(0, last + 1, drain, 0)


def per_device(queries, keys, values, out_weight):
    dma = pltpu.SemaphoreType.DMA
    block = pltpu.VMEM((ROWS, WIDE), BF16)
    state = pltpu.VMEM((HD, HD), F32)
    small = pltpu.VMEM((HD, HD), BF16)
    scratch = [
        block, block, block, pltpu.VMEM((RING * WIDE, WIDE), BF16),
        pltpu.VMEM((ROWS, WIDE), F32), pltpu.VMEM((ROWS, WIDE), F32),
        pltpu.VMEM((RING, ROWS, WIDE), BF16),
        state, state, state, state, pltpu.VMEM((3, HD, HD), F32),
        state, pltpu.VMEM((3, HD, HD), F32),
        small, small, small, pltpu.VMEM((WIDE, WIDE), BF16),
        dma((4,)), dma, dma, dma((3,)), dma((3,)), dma((3,)), dma((3,)), dma((2,)),
    ] + [dma((RING // 2,))] * 8
    return pl.pallas_call(
        kernel,
        out_shape=jax.ShapeDtypeStruct((ROWS, WIDE), BF16),
        in_specs=[pl.BlockSpec(memory_space=pl.ANY)] * 4,
        out_specs=pl.BlockSpec(memory_space=pltpu.VMEM),
        scratch_shapes=scratch,
        compiler_params=pltpu.CompilerParams(
            collective_id=0, has_side_effects=True, vmem_limit_bytes=48 * 1024 * 1024
        ),
        name="prefix_ring",
    )(queries, keys, values, out_weight)


def solution(mesh):
    return jax.shard_map(
        per_device,
        mesh=mesh,
        in_specs=(P("seq", "head"), P("seq", "head"), P("seq", "head"), P(None, "head")),
        out_specs=P("seq", "head"),
        check_vma=False,
    )
```

time: 230 us -> 121 us (0.53)
  waiting for transfers between devices: 167 us -> 0 us
  Pallas kernels: 0 us -> 115 us
  other arithmetic: 30.7 us -> 0 us
  matrix products: 15.6 us -> 0 us
  between operations: 13.5 us -> 0.01 us
  local copies, waits for them, and re-layouts: 1.41 us -> 5.51 us
    all_gather x2 -> x0, waiting for transfers between devices: 167 us -> none  [the longest x1 105 us: per_device(): lax.all_gather(mixed_heads, 'head', axis=1, tiled=True)]
    pallas_call x0 -> x1, Pallas kernels: none -> 115 us  [per_device(): pl.pallas_call(kernel, out_shape=jax.ShapeDtypeStruct((ROWS, WIDE), BF16)...]
    select_n x31 -> x0, other arithmetic: 29.4 us -> none  [step(): return jnp.where(position < mine, longer, running)]
    dot_general x4 -> x0, matrix products: 15.6 us -> none  [the longest x1 6.55 us: per_device(): jnp.dot(lax.all_gather(mixed_heads, 'head', axis=1, tiled=True), out_weig...]
    unnamed x6 -> x9, local copies, waits for them, and re-layouts: 0.01 us -> 5.51 us
  transfers between devices with their start and end apart: 2 -> 0, of which waited for: 2 -> 0; matrix products, arithmetic and copies ran while one was open for 2% -> 0% of each run, Pallas kernels for 0% -> 0%
where the time goes in v1:
time: 121 us
  Pallas kernels  115 us (95%)
  local copies, waits for them, and re-layouts  5.51 us (5%)
    pallas_call x1, Pallas kernels, per_device(): pl.pallas_call(kernel, out_shape=jax.ShapeDtypeStruct((ROWS, WIDE), BF16)...  115 us
    unnamed x9, local copies, waits for them, and re-layouts  5.51 us

profile of v1, /device:TPU:1, one launch (start us, length us, event | category | flops | bytes accessed | tf_op | source)
XLA Modules:
  0.0 120.6 jit_solution(9319449304332057462)
XLA Ops:
  0.0 0.0 copy-start
  0.0 1.6 %copy-done = bf16[4096,256]{1,0:T(8,128)(2,1)S(1)} copy-done((bf16[4096,256]{1,0:T(8,128)(2,1)S(1)}, bf16[4096,256]{1,0:T(8,128)(2,1)}, u32[]{:S(2)}) %copy-start) | copy-done | bytes 2097176
  1.6 0.0 copy-start.1
  1.6 1.0 copy-done.1
  2.6 0.0 copy-start.2
  2.6 1.0 copy-done.2
  3.7 0.0 copy-start.3
  3.7 1.0 copy-done.3
  4.7 115.0 %prefix_ring.1 = bf16[1024,256]{1,0:T(8,128)(2,1)S(1)} custom-call(bf16[1024,256]{1,0:T(8,128)(2,1)S(1)} %copy-done.1, bf16[1024,256]{1,0:T(8,128)(2,1)S(1)} %copy-done.2, bf16[1024,256]{1,0:T(8,128)(2,1)S(1)} %copy-done.3, bf16[4096,256]{1,0:T(8,128)(2,1)S(1)} %copy-done), custom_call_target="tpu_custom_call" | custom-call | tf_op jit(solution)/shard_map/prefix_ring/pallas_call | solution.py:233
  119.8 0.8 copy.6
Async XLA Ops:
  0.0 1.6 %copy-start = (bf16[4096,256]{1,0:T(8,128)(2,1)S(1)}, bf16[4096,256]{1,0:T(8,128)(2,1)}, u32[]{:S(2)}) copy-start(bf16[4096,256]{1,0:T(8,128)(2,1)} %w_hbm.1) | copy-start | bytes 6291460
  1.6 1.0 copy-start.1
  2.6 1.0 copy-start.2
  3.7 1.0 copy-start.3

commit v2 on v1

--- a/solution.py
+++ b/solution.py
@@ -11,7 +11,8 @@
 WIDE = 256
 SUB = 256
 RING = 16
-SIDE = 4
+GROUP = 32
+SHARE = 8
 F32 = jnp.float32
 BF16 = jnp.bfloat16
 
@@ -34,22 +35,26 @@
 def kernel(
     q_hbm, k_hbm, v_hbm, w_hbm, out,
     q, k, v, w, intra, acc, mixed,
-    s_own, s_send, s_recv, t_own, t_recv, r_own, r_recv, c_own, c_send, c_recv, c_blk,
-    in_sems, pair_send, pair_recv, y_send, y_recv, x_send, x_recv, c_sems,
+    shares, gathered, sums, carried, c_blk,
+    in_sems, s_send, s_recv, c_send, c_recv,
     ra_send, ra_recv, rb_send, rb_recv, la_send, la_recv, lb_send, lb_recv,
 ):
     seq, z = lax.axis_index("seq"), lax.axis_index("head")
-    core, y, x = seq % 2, (seq // 2) % SIDE, seq // (2 * SIDE)
-    partner = {"seq": seq + 1 - 2 * core}
-    y_peers = [{"seq": (x * SIDE + (y + d) % SIDE) * 2 + core} for d in range(1, SIDE)]
-    x_peers = [{"seq": (((x + d) % SIDE) * SIDE + y) * 2 + core} for d in range(1, SIDE)]
     right = {"head": (z + 1) % RING}
     left = {"head": (z + RING - 1) % RING}
 
     barrier = pltpu.get_barrier_semaphore()
-    everyone = [partner, right, left] + y_peers + x_peers
-    for who in everyone:
+
+    def greet(who):
         pl.semaphore_signal(barrier, inc=1, device_id=who, device_id_type=pl.DeviceIdType.MESH)
+
+    def greet_peer(ahead, carry):
+        greet({"seq": (seq + ahead) % GROUP})
+        return carry
+
+    greet(right)
+    greet(left)
+    lax.fori_loop(1, GROUP, greet_peer, 0)
     loads = [
         pltpu.make_async_copy(src, dst, in_sems.at[i])
         for i, (src, dst) in enumerate(((k_hbm, k), (v_hbm, v), (q_hbm, q), (w_hbm, w)))
@@ -60,11 +65,38 @@
     loads[1].wait()
     states = lax.dot_general(k[...], v[...], (((0,), (0,)), ((), ())), preferred_element_type=F32)
     first, second = states[:HD, :HD], states[HD:, HD:]
-    s_own[...] = jnp.where(core == 0, first, second)
-    s_send[...] = jnp.where(core == 0, second, first)
-    pl.semaphore_wait(barrier, len(everyone))
-    pair = remote(s_send, s_recv, pair_send, pair_recv, partner)
-    pair.start()
+    shares[pl.ds(0, GROUP // 2)] = states[:HD, :HD].reshape(GROUP // 2, SHARE, HD)
+    shares[pl.ds(GROUP // 2, GROUP // 2)] = states[HD:, HD:].reshape(GROUP // 2, SHARE, HD)
+    pl.semaphore_wait(barrier, GROUP + 1)
+
+    def outgoing(ahead):
+        peer = (seq + ahead) % GROUP
+        return remote(
+            shares.at[peer], gathered.at[seq], s_send.at[ahead], s_recv.at[ahead], {"seq": peer}
+        )
+
+    def returning(ahead):
+        peer = (seq + ahead) % GROUP
+        return remote(
+            sums.at[peer], carried.at[seq], c_send.at[ahead], c_recv.at[ahead], {"seq": peer}
+        )
+
+    def start_all(copy):
+        def body(ahead, carry):
+            copy(ahead).start()
+            return carry
+
+        lax.fori_loop(1, GROUP, body, 0)
+
+    def wait_all(copy):
+        def body(ahead, carry):
+            copy(ahead).wait()
+            return carry
+
+        lax.fori_loop(1, GROUP, body, 0)
+
+    start_all(outgoing)
+    gathered[seq] = shares[seq]
 
     def intra_part(head, part):
         cols = pl.ds(head * HD, HD)
@@ -80,54 +112,24 @@
         intra[rows, cols] = dot(scores, v[pl.ds(0, width), cols])
 
     loads[2].wait()
-    intra_part(0, 0)
-    intra_part(1, 0)
-
-    pair.wait()
-    t_own[...] = s_own[...] + s_recv[...]
-    y_copies = [
-        remote(t_own, t_recv.at[d], y_send.at[d], y_recv.at[d], y_peers[d]) for d in range(3)
-    ]
-    for copy in y_copies:
-        copy.start()
-    intra_part(0, 1)
-    intra_part(1, 1)
+    for head in range(2):
+        for part in range(2):
+            intra_part(head, part)
+    wait_all(outgoing)
+    running = jnp.zeros((SHARE, HD), F32)
+    for source in range(GROUP):
+        sums[source] = running.astype(sums.dtype)
+        running = running + gathered[source]
+    start_all(returning)
+    carried[seq] = sums[seq]
+    c_blk[...] = jnp.zeros((WIDE, WIDE), BF16)
     intra_part(0, 2)
-    for copy in y_copies:
-        copy.wait()
-    prefix = jnp.zeros((HD, HD), F32)
-    total = t_own[...]
-    for d in range(3):
-        piece = t_recv[d]
-        total = total + piece
-        prefix = prefix + jnp.where(d + 1 <= y, piece, 0.0)
-    r_own[...] = total
-    x_copies = [
-        remote(r_own, r_recv.at[d], x_send.at[d], x_recv.at[d], x_peers[d]) for d in range(3)
-    ]
-    for copy in x_copies:
-        copy.start()
-    s_send[...] = prefix
     intra_part(1, 2)
-    intra_part(0, 3)
-    intra_part(1, 3)
-    for copy in x_copies:
-        copy.wait()
-    prefix = s_send[...]
-    for d in range(3):
-        prefix = prefix + jnp.where(d + 1 <= x, r_recv[d], 0.0)
-    from_first = jnp.where(core == 0, s_own[...], s_recv[...])
-    longer = prefix + from_first
-    c_send[...] = jnp.where(core == 0, longer, prefix).astype(BF16)
-    cross = remote(c_send, c_recv, c_sems.at[0], c_sems.at[1], partner)
-    cross.start()
-    c_own[...] = jnp.where(core == 0, prefix, longer).astype(BF16)
-    c_blk[...] = jnp.zeros((WIDE, WIDE), BF16)
     loads[3].wait()
-    cross.wait()
-    mine, other = c_own[...].astype(F32), c_recv[...].astype(F32)
-    c_blk[pl.ds(0, HD), pl.ds(0, HD)] = jnp.where(core == 0, mine, other).astype(BF16)
-    c_blk[pl.ds(HD, HD), pl.ds(HD, HD)] = jnp.where(core == 0, other, mine).astype(BF16)
+    wait_all(returning)
+    for head in range(2):
+        mine = carried[pl.ds(head * GROUP // 2, GROUP // 2)].astype(F32).reshape(HD, HD)
+        c_blk[pl.ds(head * HD, HD), pl.ds(head * HD, HD)] = mine.astype(BF16)
 
     def piece_at(owner, half):
         return mixed.at[owner, pl.ds(half * HALF, HALF)]
@@ -160,6 +162,8 @@
     norm_half(0)
     right_a(0).start()
     left_a(0).start()
+    intra_part(0, 3)
+    intra_part(1, 3)
     norm_half(1)
     left_b(0).start()
     right_b(0).start()
@@ -219,16 +223,14 @@
 def per_device(queries, keys, values, out_weight):
     dma = pltpu.SemaphoreType.DMA
     block = pltpu.VMEM((ROWS, WIDE), BF16)
-    state = pltpu.VMEM((HD, HD), F32)
-    small = pltpu.VMEM((HD, HD), BF16)
+    share = pltpu.VMEM((GROUP, SHARE, HD), F32)
+    small = pltpu.VMEM((GROUP, SHARE, HD), BF16)
     scratch = [
         block, block, block, pltpu.VMEM((RING * WIDE, WIDE), BF16),
         pltpu.VMEM((ROWS, WIDE), F32), pltpu.VMEM((ROWS, WIDE), F32),
         pltpu.VMEM((RING, ROWS, WIDE), BF16),
-        state, state, state, state, pltpu.VMEM((3, HD, HD), F32),
-        state, pltpu.VMEM((3, HD, HD), F32),
-        small, small, small, pltpu.VMEM((WIDE, WIDE), BF16),
-        dma((4,)), dma, dma, dma((3,)), dma((3,)), dma((3,)), dma((3,)), dma((2,)),
+        share, share, small, small, pltpu.VMEM((WIDE, WIDE), BF16),
+        dma((4,)), dma((GROUP,)), dma((GROUP,)), dma((GROUP,)), dma((GROUP,)),
     ] + [dma((RING // 2,))] * 8
     return pl.pallas_call(
         kernel,
@@ -237,7 +239,7 @@
         out_specs=pl.BlockSpec(memory_space=pltpu.VMEM),
         scratch_shapes=scratch,
         compiler_params=pltpu.CompilerParams(
-            collective_id=0, has_side_effects=True, vmem_limit_bytes=48 * 1024 * 1024
+            collective_id=0, has_side_effects=True, vmem_limit_bytes=67_043_328
         ),
         name="prefix_ring",
     )(queries, keys, values, out_weight)

time: 121 us -> 118 us (0.975)
  local copies, waits for them, and re-layouts: 5.51 us -> 1.87 us
    unnamed x9 -> x1, local copies, waits for them, and re-layouts: 5.51 us -> 1.87 us
where the time goes in v2:
time: 118 us
  Pallas kernels  116 us (98%)
  local copies, waits for them, and re-layouts  1.87 us (2%)
    pallas_call x1, Pallas kernels, per_device(): pl.pallas_call(kernel, out_shape=jax.ShapeDtypeStruct((ROWS, WIDE), BF16)...  116 us

profile of v2, /device:TPU:1, one launch (start us, length us, event | category | flops | bytes accessed | tf_op | source)
XLA Modules:
  0.0 117.5 jit_solution(6766839226762248780)
XLA Ops:
  0.0 115.6 %prefix_ring.1 = bf16[1024,256]{1,0:T(8,128)(2,1)} custom-call(bf16[1024,256]{1,0:T(8,128)(2,1)} %q_hbm.1, bf16[1024,256]{1,0:T(8,128)(2,1)} %k_hbm.1, bf16[1024,256]{1,0:T(8,128)(2,1)} %v_hbm.1, bf16[4096,256]{1,0:T(8,128)(2,1)} %w_hbm.1), custom_call_target="tpu_custom_call" | custom-call | tf_op jit(solution)/shard_map/prefix_ring/pallas_call | solution.py:235
  115.6 1.9 %copy.6 = bf16[1024,256]{1,0:T(8,128)(2,1)} copy(bf16[1024,256]{1,0:T(8,128)(2,1)} %prefix_ring.1) | data formatting | bytes 1048576

commit v3 on v2

--- a/solution.py
+++ b/solution.py
@@ -52,19 +52,20 @@
         greet({"seq": (seq + ahead) % GROUP})
         return carry
 
-    greet(right)
-    greet(left)
-    lax.fori_loop(1, GROUP, greet_peer, 0)
     loads = [
         pltpu.make_async_copy(src, dst, in_sems.at[i])
         for i, (src, dst) in enumerate(((k_hbm, k), (v_hbm, v), (q_hbm, q), (w_hbm, w)))
     ]
-    for load in loads:
-        load.start()
+    loads[0].start()
+    loads[1].start()
+    greet(right)
+    greet(left)
+    lax.fori_loop(1, GROUP, greet_peer, 0)
     loads[0].wait()
     loads[1].wait()
+    loads[2].start()
+    loads[3].start()
     states = lax.dot_general(k[...], v[...], (((0,), (0,)), ((), ())), preferred_element_type=F32)
-    first, second = states[:HD, :HD], states[HD:, HD:]
     shares[pl.ds(0, GROUP // 2)] = states[:HD, :HD].reshape(GROUP // 2, SHARE, HD)
     shares[pl.ds(GROUP // 2, GROUP // 2)] = states[HD:, HD:].reshape(GROUP // 2, SHARE, HD)
     pl.semaphore_wait(barrier, GROUP + 1)
@@ -235,14 +236,14 @@
     return pl.pallas_call(
         kernel,
         out_shape=jax.ShapeDtypeStruct((ROWS, WIDE), BF16),
-        in_specs=[pl.BlockSpec(memory_space=pl.ANY)] * 4,
+        in_specs=[pl.BlockSpec(memory_space=pltpu.HBM)] * 4,
         out_specs=pl.BlockSpec(memory_space=pltpu.VMEM),
         scratch_shapes=scratch,
         compiler_params=pltpu.CompilerParams(
-            collective_id=0, has_side_effects=True, vmem_limit_bytes=67_043_328
+            collective_id=0, has_side_effects=True, vmem_limit_bytes=32 * 1024 * 1024
         ),
         name="prefix_ring",
-    )(queries, keys, values, out_weight)
+    )(*(pltpu.with_memory_space_constraint(a, pltpu.HBM) for a in (queries, keys, values, out_weight)))
 
 
 def solution(mesh):

time: 118 us -> 116 us (0.983)
  no operation moved by 1% of the time
where the time goes in v3:
time: 116 us
  Pallas kernels  115 us (99%)
    pallas_call x1, Pallas kernels, per_device(): pl.pallas_call(kernel, out_shape=jax.ShapeDtypeStruct((ROWS, WIDE), BF16)...  115 us

profile of v3, /device:TPU:1, one launch (start us, length us, event | category | flops | bytes accessed | tf_op | source)
XLA Modules:
  0.0 115.6 jit_solution(10404790611385864809)
XLA Ops:
  0.0 114.8 %prefix_ring.1 = bf16[1024,256]{1,0:T(8,128)(2,1)S(1)} custom-call(bf16[1024,256]{1,0:T(8,128)(2,1)} %q_hbm.1, bf16[1024,256]{1,0:T(8,128)(2,1)} %k_hbm.1, bf16[1024,256]{1,0:T(8,128)(2,1)} %v_hbm.1, bf16[4096,256]{1,0:T(8,128)(2,1)} %w_hbm.1), custom_call_target="tpu_custom_call" | custom-call | tf_op jit(solution)/shard_map/prefix_ring/pallas_call | solution.py:236
  114.8 0.8 copy.6

commit v4 on v3

--- a/solution.py
+++ b/solution.py
@@ -37,7 +37,7 @@
     q, k, v, w, intra, acc, mixed,
     shares, gathered, sums, carried, c_blk,
     in_sems, s_send, s_recv, c_send, c_recv,
-    ra_send, ra_recv, rb_send, rb_recv, la_send, la_recv, lb_send, lb_recv,
+    r_send, r_recv, l_send, l_recv,
 ):
     seq, z = lax.axis_index("seq"), lax.axis_index("head")
     right = {"head": (z + 1) % RING}
@@ -132,42 +132,26 @@
         mine = carried[pl.ds(head * GROUP // 2, GROUP // 2)].astype(F32).reshape(HD, HD)
         c_blk[pl.ds(head * HD, HD), pl.ds(head * HD, HD)] = mine.astype(BF16)
 
-    def piece_at(owner, half):
-        return mixed.at[owner, pl.ds(half * HALF, HALF)]
-
-    def hop(owner, half, send, recv, step, where):
-        ref = piece_at(owner, half)
-        return remote(ref, ref, send.at[step], recv.at[step], where)
-
-    def right_a(step):
-        return hop((z + RING - step) % RING, 0, ra_send, ra_recv, step, right)
-
-    def right_b(step):
-        return hop((z + RING - step) % RING, 1, rb_send, rb_recv, step, right)
-
-    def left_a(step):
-        return hop((z + step) % RING, 0, la_send, la_recv, step, left)
-
-    def left_b(step):
-        return hop((z + step) % RING, 1, lb_send, lb_recv, step, left)
-
-    def norm_half(half):
-        for part in range(2):
-            rows = pl.ds(half * HALF + part * SUB, SUB)
-            attended = intra[rows, :] + dot(q[rows, :], c_blk[...])
-            for head in range(2):
-                own = attended[:, head * HD:(head + 1) * HD]
-                scale = lax.rsqrt(jnp.mean(own * own, -1, keepdims=True) + 1e-06)
-                mixed[z, rows, pl.ds(head * HD, HD)] = (own * scale).astype(BF16)
-
-    norm_half(0)
-    right_a(0).start()
-    left_a(0).start()
-    intra_part(0, 3)
-    intra_part(1, 3)
-    norm_half(1)
-    left_b(0).start()
-    right_b(0).start()
+    def to_right(part, step):
+        ref = mixed.at[(z + RING - step) % RING, pl.ds(part * SUB, SUB)]
+        return remote(ref, ref, r_send.at[part, step], r_recv.at[part, step], right)
+
+    def to_left(part, step):
+        ref = mixed.at[(z + step) % RING, pl.ds(part * SUB, SUB)]
+        return remote(ref, ref, l_send.at[part, step], l_recv.at[part, step], left)
+
+    for part in range(4):
+        if part == 3:
+            intra_part(0, 3)
+            intra_part(1, 3)
+        rows = pl.ds(part * SUB, SUB)
+        attended = intra[rows, :] + dot(q[rows, :], c_blk[...])
+        for head in range(2):
+            own = attended[:, head * HD:(head + 1) * HD]
+            scale = lax.rsqrt(jnp.mean(own * own, -1, keepdims=True) + 1e-06)
+            mixed[z, rows, pl.ds(head * HD, HD)] = (own * scale).astype(BF16)
+        to_right(part, 0).start()
+        to_left(part, 0).start()
 
     def weights(owner):
         return w[pl.ds(pl.multiple_of(owner * WIDE, WIDE), WIDE), :]
@@ -178,43 +162,44 @@
         rows = pl.ds(half * HALF, HALF)
         acc[rows, :] += dot(mixed[owner, rows, :], weights(owner))
 
+    far_pieces = ((to_right, 0), (to_left, 2), (to_right, 1), (to_left, 3))
+    near_pieces = ((to_left, 0), (to_right, 2), (to_left, 1), (to_right, 3))
+    last = RING // 2 - 1
+
     def step_body(step, carry):
         before = (z + 2 * RING - step - 1) % RING
         after = (z + step + 1) % RING
-        right_a(step).wait_recv()
-        right_a(step + 1).start()
-        left_b(step).wait_recv()
-        left_b(step + 1).start()
+        for copy, part in far_pieces:
+            copy(part, step).wait_recv()
+            copy(part, step + 1).start()
         add(before, 0)
         add(after, 1)
-        left_a(step).wait_recv()
-        right_b(step).wait_recv()
-
-        @pl.when(step < RING // 2 - 2)
-        def _():
-            left_a(step + 1).start()
-            right_b(step + 1).start()
+        for copy, part in near_pieces:
+            copy(part, step).wait_recv()
+
+            @pl.when(step < last - 1)
+            def _():
+                copy(part, step + 1).start()
 
         add(after, 0)
         add(before, 1)
         return carry
 
-    last = RING // 2 - 1
     lax.fori_loop(0, last, step_body, 0)
     far = (z + RING // 2) % RING
-    for half, copy in ((0, right_a(last)), (1, left_b(last))):
-        copy.wait_recv()
-        rows = pl.ds(half * HALF, HALF)
+    for copy, part in far_pieces:
+        copy(part, last).wait_recv()
+        rows = pl.ds(part * SUB, SUB)
         out[rows, :] = (acc[rows, :] + dot(mixed[far, rows, :], weights(far))).astype(BF16)
 
     def drain(step, carry):
-        right_a(step).wait_send()
-        left_b(step).wait_send()
+        for copy, part in far_pieces:
+            copy(part, step).wait_send()
 
         @pl.when(step < last)
         def _():
-            left_a(step).wait_send()
-            right_b(step).wait_send()
+            for copy, part in near_pieces:
+                copy(part, step).wait_send()
 
         return carry
 
@@ -232,7 +217,7 @@
         pltpu.VMEM((RING, ROWS, WIDE), BF16),
         share, share, small, small, pltpu.VMEM((WIDE, WIDE), BF16),
         dma((4,)), dma((GROUP,)), dma((GROUP,)), dma((GROUP,)), dma((GROUP,)),
-    ] + [dma((RING // 2,))] * 8
+    ] + [dma((4, RING // 2))] * 4
     return pl.pallas_call(
         kernel,
         out_shape=jax.ShapeDtypeStruct((ROWS, WIDE), BF16),

time: 116 us -> 116 us (level)
  no operation moved by 1% of the time
where the time goes in v4:
time: 116 us
  Pallas kernels  115 us (99%)
    pallas_call x1, Pallas kernels, per_device(): pl.pallas_call(kernel, out_shape=jax.ShapeDtypeStruct((ROWS, WIDE), BF16)...  115 us

profile of v4, /device:TPU:1, one launch (start us, length us, event | category | flops | bytes accessed | tf_op | source)
XLA Modules:
  0.0 116.0 jit_solution(11610774655918244842)
XLA Ops:
  0.0 115.2 %prefix_ring.1 = bf16[1024,256]{1,0:T(8,128)(2,1)S(1)} custom-call(bf16[1024,256]{1,0:T(8,128)(2,1)} %q_hbm.1, bf16[1024,256]{1,0:T(8,128)(2,1)} %k_hbm.1, bf16[1024,256]{1,0:T(8,128)(2,1)} %v_hbm.1, bf16[4096,256]{1,0:T(8,128)(2,1)} %w_hbm.1), custom_call_target="tpu_custom_call" | custom-call | tf_op jit(solution)/shard_map/prefix_ring/pallas_call | solution.py:221
  115.2 0.8 copy.6

commit v5 on v4

--- a/solution.py
+++ b/solution.py
@@ -37,7 +37,7 @@
     q, k, v, w, intra, acc, mixed,
     shares, gathered, sums, carried, c_blk,
     in_sems, s_send, s_recv, c_send, c_recv,
-    r_send, r_recv, l_send, l_recv,
+    r_send, r_recv,
 ):
     seq, z = lax.axis_index("seq"), lax.axis_index("head")
     right = {"head": (z + 1) % RING}
@@ -132,13 +132,15 @@
         mine = carried[pl.ds(head * GROUP // 2, GROUP // 2)].astype(F32).reshape(HD, HD)
         c_blk[pl.ds(head * HD, HD), pl.ds(head * HD, HD)] = mine.astype(BF16)
 
-    def to_right(part, step):
-        ref = mixed.at[(z + RING - step) % RING, pl.ds(part * SUB, SUB)]
-        return remote(ref, ref, r_send.at[part, step], r_recv.at[part, step], right)
-
-    def to_left(part, step):
-        ref = mixed.at[(z + step) % RING, pl.ds(part * SUB, SUB)]
-        return remote(ref, ref, l_send.at[part, step], l_recv.at[part, step], left)
+    core = seq % 2
+    onward = {"head": (z + 1 + core * (RING - 2)) % RING}
+
+    def owner_at(step):
+        return (z + 2 * RING + step * (2 * core - 1)) % RING
+
+    def piece(part, step):
+        ref = mixed.at[owner_at(step), pl.ds(part * SUB, SUB)]
+        return remote(ref, ref, r_send.at[part, step], r_recv.at[part, step], onward)
 
     for part in range(4):
         if part == 3:
@@ -150,8 +152,7 @@
             own = attended[:, head * HD:(head + 1) * HD]
             scale = lax.rsqrt(jnp.mean(own * own, -1, keepdims=True) + 1e-06)
             mixed[z, rows, pl.ds(head * HD, HD)] = (own * scale).astype(BF16)
-        to_right(part, 0).start()
-        to_left(part, 0).start()
+        piece(part, 0).start()
 
     def weights(owner):
         return w[pl.ds(pl.multiple_of(owner * WIDE, WIDE), WIDE), :]
@@ -162,45 +163,27 @@
         rows = pl.ds(half * HALF, HALF)
         acc[rows, :] += dot(mixed[owner, rows, :], weights(owner))
 
-    far_pieces = ((to_right, 0), (to_left, 2), (to_right, 1), (to_left, 3))
-    near_pieces = ((to_left, 0), (to_right, 2), (to_left, 1), (to_right, 3))
-    last = RING // 2 - 1
+    last = RING - 2
 
     def step_body(step, carry):
-        before = (z + 2 * RING - step - 1) % RING
-        after = (z + step + 1) % RING
-        for copy, part in far_pieces:
-            copy(part, step).wait_recv()
-            copy(part, step + 1).start()
-        add(before, 0)
-        add(after, 1)
-        for copy, part in near_pieces:
-            copy(part, step).wait_recv()
-
-            @pl.when(step < last - 1)
-            def _():
-                copy(part, step + 1).start()
-
-        add(after, 0)
-        add(before, 1)
+        owner = owner_at(step + 1)
+        for half in range(2):
+            for part in (2 * half, 2 * half + 1):
+                piece(part, step).wait_recv()
+                piece(part, step + 1).start()
+            add(owner, half)
         return carry
 
     lax.fori_loop(0, last, step_body, 0)
-    far = (z + RING // 2) % RING
-    for copy, part in far_pieces:
-        copy(part, last).wait_recv()
+    far = owner_at(RING - 1)
+    for part in range(4):
+        piece(part, last).wait_recv()
         rows = pl.ds(part * SUB, SUB)
         out[rows, :] = (acc[rows, :] + dot(mixed[far, rows, :], weights(far))).astype(BF16)
 
     def drain(step, carry):
-        for copy, part in far_pieces:
-            copy(part, step).wait_send()
-
-        @pl.when(step < last)
-        def _():
-            for copy, part in near_pieces:
-                copy(part, step).wait_send()
-
+        for part in range(4):
+            piece(part, step).wait_send()
         return carry
 
     lax.fori_loop(0, last + 1, drain, 0)
@@ -217,7 +200,7 @@
         pltpu.VMEM((RING, ROWS, WIDE), BF16),
         share, share, small, small, pltpu.VMEM((WIDE, WIDE), BF16),
         dma((4,)), dma((GROUP,)), dma((GROUP,)), dma((GROUP,)), dma((GROUP,)),
-    ] + [dma((4, RING // 2))] * 4
+    ] + [dma((4, RING - 1))] * 2
     return pl.pallas_call(
         kernel,
         out_shape=jax.ShapeDtypeStruct((ROWS, WIDE), BF16),

time: 116 us -> 115 us (level)
  the two profiles are of different devices: /device:TPU:1 before, /device:TPU:8 now
where the time goes in v5:
time: 115 us
  Pallas kernels  114 us (99%)
    pallas_call x1, Pallas kernels, per_device(): pl.pallas_call(kernel, out_shape=jax.ShapeDtypeStruct((ROWS, WIDE), BF16)...  114 us

profile of v5, /device:TPU:8, one launch (start us, length us, event | category | flops | bytes accessed | tf_op | source)
XLA Modules:
  0.0 115.0 jit_solution(17107645866706488636)
XLA Ops:
  0.0 114.2 %prefix_ring.1 = bf16[1024,256]{1,0:T(8,128)(2,1)S(1)} custom-call(bf16[1024,256]{1,0:T(8,128)(2,1)} %q_hbm.1, bf16[1024,256]{1,0:T(8,128)(2,1)} %k_hbm.1, bf16[1024,256]{1,0:T(8,128)(2,1)} %v_hbm.1, bf16[4096,256]{1,0:T(8,128)(2,1)} %w_hbm.1), custom_call_target="tpu_custom_call" | custom-call | tf_op jit(solution)/shard_map/prefix_ring/pallas_call | solution.py:204
  114.2 0.8 copy.6

commit v6 on v3

--- a/solution.py
+++ b/solution.py
@@ -197,28 +197,26 @@
 
         add(after, 0)
         add(before, 1)
+
+        @pl.when(step > 0)
+        def _():
+            for copy in (right_a, left_b, left_a, right_b):
+                copy(step - 1).wait_send()
+
         return carry
 
     last = RING // 2 - 1
     lax.fori_loop(0, last, step_body, 0)
+    for copy in (right_a, left_b, left_a, right_b):
+        copy(last - 1).wait_send()
     far = (z + RING // 2) % RING
     for half, copy in ((0, right_a(last)), (1, left_b(last))):
         copy.wait_recv()
         rows = pl.ds(half * HALF, HALF)
         out[rows, :] = (acc[rows, :] + dot(mixed[far, rows, :], weights(far))).astype(BF16)
 
-    def drain(step, carry):
-        right_a(step).wait_send()
-        left_b(step).wait_send()
-
-        @pl.when(step < last)
-        def _():
-            left_a(step).wait_send()
-            right_b(step).wait_send()
-
-        return carry
-
-    lax.fori_loop(0, last + 1, drain, 0)
+    right_a(last).wait_send()
+    left_b(last).wait_send()
 
 
 def per_device(queries, keys, values, out_weight):

time: 116 us -> 116 us (level)
  no operation moved by 1% of the time
where the time goes in v6:
time: 116 us
  Pallas kernels  115 us (99%)
    pallas_call x1, Pallas kernels, per_device(): pl.pallas_call(kernel, out_shape=jax.ShapeDtypeStruct((ROWS, WIDE), BF16)...  115 us

profile of v6, /device:TPU:1, one launch (start us, length us, event | category | flops | bytes accessed | tf_op | source)
XLA Modules:
  0.0 115.6 jit_solution(15458382609311088111)
XLA Ops:
  0.0 114.8 %prefix_ring.1 = bf16[1024,256]{1,0:T(8,128)(2,1)S(1)} custom-call(bf16[1024,256]{1,0:T(8,128)(2,1)} %q_hbm.1, bf16[1024,256]{1,0:T(8,128)(2,1)} %k_hbm.1, bf16[1024,256]{1,0:T(8,128)(2,1)} %v_hbm.1, bf16[4096,256]{1,0:T(8,128)(2,1)} %w_hbm.1), custom_call_target="tpu_custom_call" | custom-call | tf_op jit(solution)/shard_map/prefix_ring/pallas_call | solution.py:234
  114.8 0.8 copy.6
